TPU v7x, 256 devices: a whole 4x4x8 slice. The times are simulated.
256 devices in a mesh: row: 16 (over x_hi, z), col: 16 (over y, x_lo, core).
Axes of the slice: x: 4 (x_hi: 2, x_lo: 2; x = x_hi * 2 + x_lo), y: 4, z: 8, core: 2. Of those that a mesh axis runs over, the one named last changes fastest.
Arguments:
- panel_values: bfloat16 [65536, 256], P(('row', 'col')), may hold values from -6 to 6
- near_tiles: bfloat16 [8192, 256, 256], P(('row', 'col')), may hold values from -0.01953125 to 0.01953125
- far_left: bfloat16 [32768, 64, 256], P(('row', 'col')), may hold values from -0.0390625 to 0.0390625
- far_right: bfloat16 [32768, 64, 256], P(('row', 'col')), may hold values from -0.375 to 0.375
- near_rows: int32 [8192], P(('row', 'col')), may hold values from 0 to 255, as said below
- far_rows: int32 [32768], P(('row', 'col')), may hold values from 0 to 255, as said below
Outputs:
- panel_product: bfloat16 [65536, 256], P(('row', 'col'))
Inputs may be any that keep to these rules, and one draw needn't show every extreme that they name: `near_rows`: entries of the device at grid position (i, j) lie in its row group, clusters i * 16 * 1 to (i + 1) * 16 - 1. `far_rows`: entries of the device at grid position (i, j) lie in its row group, clusters i * 16 * 1 to (i + 1) * 16 - 1.
All inputs are finite; a program needn't handle non-finite values.
Results may differ from a plain program's by a relative error of at most 0.0046.
Values may be sent and summed in bfloat16 or wider, within the bound.
A program may use at most 192 MiB of HBM per device.

v0:
```python
import jax
import jax.numpy as jnp
from jax import lax
from jax.sharding import PartitionSpec as P

TILE = 256
RANK = 64
NRHS = 256
DPC = 2
LPC = 8


def back_part(near_tiles, far_left, far_right, near_input, far_input, count):
    near_out = jnp.einsum(
        "sij,sin->sjn", near_tiles, near_input, preferred_element_type=jnp.float32
    )
    near_sum = near_out.reshape(count, DPC, TILE, NRHS).sum(axis=1)
    coef = jnp.einsum(
        "skt,stn->skn", far_left, far_input, preferred_element_type=jnp.float32
    ).astype(jnp.bfloat16)
    far_out = jnp.einsum("skt,skn->stn", far_right, coef, preferred_element_type=jnp.float32)
    far_sum = far_out.reshape(count, LPC, TILE, NRHS).sum(axis=1)
    return (near_sum + far_sum).reshape(count * TILE, NRHS)


def forward_part(near_tiles, far_left, far_right, near_local, far_local, colx, count, groups):
    tiles = near_tiles.reshape(count, DPC, TILE, TILE)
    near_out = jnp.einsum("cdij,cjn->cdin", tiles, colx, preferred_element_type=jnp.float32)
    near_out = near_out.reshape(count * DPC, TILE, NRHS)
    right = far_right.reshape(count, LPC, RANK, TILE)
    coef = jnp.einsum("cdkt,ctn->cdkn", right, colx, preferred_element_type=jnp.float32).astype(
        jnp.bfloat16
    )
    left = far_left.reshape(count, LPC, RANK, TILE)
    far_out = jnp.einsum("cdkt,cdkn->cdtn", left, coef, preferred_element_type=jnp.float32)
    far_out = far_out.reshape(count * LPC, TILE, NRHS)
    total = jax.ops.segment_sum(near_out, near_local, num_segments=groups)
    total = total + jax.ops.segment_sum(far_out, far_local, num_segments=groups)
    return total.reshape(groups * TILE, NRHS)


def per_device(panel_values, near_tiles, far_left, far_right, near_rows, far_rows):
    n_row = lax.axis_size("row")
    n_col = lax.axis_size("col")
    clusters = panel_values.shape[0] // TILE
    groups = n_col * clusters
    colcount = n_row * clusters
    row_base = lax.axis_index("row") * groups
    near_local = near_rows - row_base
    far_local = far_rows - row_base
    row_slab = lax.all_gather(panel_values, "col", axis=0, tiled=True)
    rowx = row_slab.reshape(groups, TILE, NRHS)
    near_input = jnp.take(rowx, near_local, axis=0)
    far_input = jnp.take(rowx, far_local, axis=0)
    col_slab = lax.all_gather(panel_values, "row", axis=0, tiled=True)
    colx = col_slab.reshape(colcount, TILE, NRHS)
    forward = forward_part(
        near_tiles, far_left, far_right, near_local, far_local, colx, colcount, groups
    )
    backward = back_part(near_tiles, far_left, far_right, near_input, far_input, colcount)
    own_back = lax.psum_scatter(backward, "row", scatter_dimension=0, tiled=True)
    own_forward = lax.psum_scatter(forward, "col", scatter_dimension=0, tiled=True)
    return (own_forward + own_back).astype(jnp.bfloat16)


def solution(mesh):
    placed = (
        P(("row", "col"), None),
        P(("row", "col"), None, None),
        P(("row", "col"), None, None),
        P(("row", "col"), None, None),
        P(("row", "col")),
        P(("row", "col")),
    )
    return jax.shard_map(
        per_device, mesh=mesh, in_specs=placed, out_specs=P(("row", "col"), None), check_vma=False
    )
```

profile of v0, /device:TPU:32, one launch (start us, length us, event | category | flops | bytes accessed | tf_op | source)
XLA Modules:
  0.0 426.7 jit_solution(15875031635582271066)
XLA Ops:
  6.5 0.0 all-gather.5.cloned.1.call-start
  6.5 0.7 all-gather.5.cloned.1.call-update
  7.3 0.0 all-gather.3.cloned.1.call-start
  7.3 0.7 all-gather.3.cloned.1.call-update
  8.0 0.0 reduce-scatter.5.cloned.1.call-start
  8.1 0.7 compare_and_fusion
  8.7 0.7 compare_and_fusion.1
  9.4 38.9 %all-gather.5.cloned.1.call-done = bf16[4096,256]{1,0:T(8,128)(2,1)} async-done(((bf16[256,256]{1,0:T(8,128)(2,1)}), bf16[4096,256]{1,0:T(8,128)(2,1)}) %all-gather.5.cloned.1.call-update) | async-done | bytes 2097168 | tf_op jit(solution)/shard_map/all_gather | solution.py:51
  48.3 0.0 copy-start
  48.3 10.0 %gather_fusion.1 = bf16[128,256,256]{2,1,0:T(8,128)(2,1)} fusion(bf16[16,256,256]{2,1,0:T(8,128)(2,1)} %bitcast.32, s32[1024]{0:T(1024)S(1)} %pad_clamp_fusion), kind=kCustom, calls=%fused_computation.1 | custom fusion | bytes 33554944 | tf_op jit(solution)/shard_map/jit(_take)/gather | solution.py:54
  58.3 0.0 copy-done
  58.3 2.8 gather_fusion
  61.1 7.4 %bitcast_reduce_fusion.1 = f32[16,256,256]{1,2,0:T(8,128)} fusion(bf16[32,256,256]{2,1,0:T(8,128)(2,1)} %param.7, bf16[32,256,256]{2,1,0:T(8,128)(2,1)} %gather_fusion, pred[32]{0:T(512)(128)(4,1)S(1)} %get-tuple-element.7), kind=kOutput, calls=%fused_computation.8 | convolution fusion | flops 1076887552 | bytes 12582944 | tf_op jit(solution)/shard_map/sij,sin->sjn/dot_general | solution.py:14
  68.5 16.6 %bitcast_reduce_fusion = f32[16,256,256]{1,2,0:T(8,128)} fusion(bf16[128,64,256]{2,1,0:T(8,128)(2,1)} %param.9, bf16[128,64,256]{2,1,0:T(8,128)(2,1)} %param.8, bf16[128,256,256]{2,1,0:T(8,128)(2,1)} %gather_fusion.1, pred[128]{0:T(512)(128)(4,1)S(1)} %get-tuple-element.5), kind=kOutput, calls=%fused_computation.4 | convolution fusion | flops 2165309440 | bytes 29360256 | tf_op jit(solution)/shard_map/skt,skn->stn/dot_general | solution.py:21
  85.1 6.0 %add.42 = f32[16,256,256]{1,2,0:T(8,128)} add(f32[16,256,256]{1,2,0:T(8,128)} %bitcast_reduce_fusion.1, f32[16,256,256]{1,2,0:T(8,128)} %bitcast_reduce_fusion) | non-fusion elementwise | flops 1048576 | bytes 12582912 | tf_op jit(solution)/shard_map/add | solution.py:23
  91.1 5.3 %copy.13 = f32[16,256,256]{2,1,0:T(8,128)} copy(f32[16,256,256]{1,2,0:T(8,128)} %add.42) | data formatting | bytes 8388608 | tf_op jit(solution)/shard_map/add | solution.py:23
  96.4 0.0 reduce-scatter.5.cloned.1.call-update
  96.5 0.2 reduce-scatter.3.cloned.1.call-start
  96.7 39.2 %all-gather.3.cloned.1.call-done = bf16[4096,256]{1,0:T(8,128)(2,1)} async-done(((bf16[256,256]{1,0:T(8,128)(2,1)}), bf16[4096,256]{1,0:T(8,128)(2,1)}) %all-gather.3.cloned.1.call-update) | async-done | bytes 2097168 | tf_op jit(solution)/shard_map/all_gather | solution.py:55
  135.9 16.3 %fusion.16 = f32[16,8,256,256]{3,2,1,0:T(8,128)} fusion(bf16[16,8,64,256]{3,2,1,0:T(8,128)(2,1)} %bitcast.41, bf16[16,8,64,256]{3,2,1,0:T(8,128)(2,1)} %bitcast.40, bf16[16,256,256,1]{2,1,3,0:T(8,128)(2,1)} %bitcast.35), kind=kOutput, calls=%fused_computation.14 | convolution fusion | flops 2149580800 | bytes 44040192 | tf_op jit(solution)/shard_map/cdkt,cdkn->cdtn/dot_general | solution.py:35
  152.3 33.5 %copy.11 = f32[128,256,256]{2,1,0:T(8,128)} copy(f32[128,256,256]{1,2,0:T(8,128)} %bitcast.31) | data formatting | bytes 67108864 | tf_op jit(solution)/shard_map/reshape | solution.py:36
  185.8 2.5 broadcast.9.clone.1
  188.3 72.1 %scatter_fusion.1 = f32[16,256,256]{2,1,0:T(8,128)} fusion(f32[16,256,256]{2,1,0:T(8,128)} %broadcast.9.clone.1, s32[128]{0:T(128)S(1)} %get-tuple-element.6, f32[128,256,256]{2,1,0:T(8,128)} %copy.11), kind=kCustom, calls=%fused_computation.3 | custom fusion | flops 8388608 | bytes 100663808 | tf_op jit(solution)/shard_map/scatter-add | solution.py:38
  260.4 0.0 copy-done.1
  260.4 6.7 %fusion.27 = f32[16,2,256,256]{3,2,1,0:T(8,128)} fusion(bf16[16,2,256,256]{3,2,1,0:T(8,128)(2,1)} %bitcast.39, bf16[16,256,256,1]{2,1,3,0:T(8,128)(2,1)S(1)} %bitcast.36), kind=kOutput, calls=%fused_computation.30 | convolution fusion | flops 1073741824 | bytes 14680064 | tf_op jit(solution)/shard_map/cdij,cjn->cdin/dot_general | solution.py:28
  267.0 2.4 broadcast.9.clone
  269.4 18.2 %scatter_fusion = f32[16,256,256]{2,1,0:T(8,128)} fusion(f32[16,256,256]{2,1,0:T(8,128)} %broadcast.9.clone, s32[32]{0:T(128)S(1)} %get-tuple-element.8, f32[32,256,256]{2,1,0:T(8,128)} %bitcast.34), kind=kCustom, calls=%fused_computation.2 | custom fusion | flops 2097152 | bytes 25165952 | tf_op jit(solution)/shard_map/scatter-add | solution.py:37
  287.7 6.1 %add.37 = f32[16,256,256]{2,1,0:T(8,128)} add(f32[16,256,256]{2,1,0:T(8,128)} %scatter_fusion, f32[16,256,256]{2,1,0:T(8,128)} %scatter_fusion.1) | non-fusion elementwise | flops 1048576 | bytes 12582912 | tf_op jit(solution)/shard_map/add | solution.py:38
  293.7 0.0 reduce-scatter.3.cloned.1.call-update
  293.8 51.1 %reduce-scatter.5.cloned.1.call-done = f32[256,256]{1,0:T(8,128)} async-done(((f32[4096,256]{1,0:T(8,128)}), f32[256,256]{1,0:T(8,128)}) %reduce-scatter.5.cloned.1.call-update) | async-done | bytes 262160 | tf_op jit(solution)/shard_map/reduce_scatter | solution.py:61
  344.9 73.6 %reduce-scatter.3.cloned.1.call-done = f32[256,256]{1,0:T(8,128)} async-done(((f32[4096,256]{1,0:T(8,128)}), f32[256,256]{1,0:T(8,128)}) %reduce-scatter.3.cloned.1.call-update) | async-done | bytes 262160 | tf_op jit(solution)/shard_map/reduce_scatter | solution.py:62
  418.4 1.7 add_convert_fusion
  (5 shorter events, 0.0 us)
Async XLA Ops:
  6.5 41.8 %all-gather.5.cloned.1.call-start = ((), (), s32[]{:S(2)}) async-start(), calls=%async_computation.4 | async-start | bytes 2228224 | tf_op jit(solution)/shard_map/all_gather | solution.py:51
  7.3 128.7 %all-gather.3.cloned.1.call-start = ((), (), s32[]{:S(2)}) async-start(), calls=%async_computation.2 | async-start | bytes 2228224 | tf_op jit(solution)/shard_map/all_gather | solution.py:55
  8.0 336.9 %reduce-scatter.5.cloned.1.call-start = ((), (), s32[]{:S(2)}) async-start(), calls=%async_computation.5 | async-start | bytes 4456448 | tf_op jit(solution)/shard_map/reduce_scatter | solution.py:61
  48.3 10.0 %copy-start = (bf16[4096,256]{1,0:T(8,128)(2,1)S(1)}, bf16[4096,256]{1,0:T(8,128)(2,1)}, u32[]{:S(2)}) copy-start(bf16[4096,256]{1,0:T(8,128)(2,1)} %all-gather.5.cloned.1.call-done) | copy-start | bytes 6291460
  96.5 322.0 %reduce-scatter.3.cloned.1.call-start = ((), (), s32[]{:S(2)}) async-start(), calls=%async_computation.3 | async-start | bytes 4456448 | tf_op jit(solution)/shard_map/reduce_scatter | solution.py:62
  188.3 72.1 %copy-start.1 = (bf16[4096,256]{1,0:T(8,128)(2,1)S(1)}, bf16[4096,256]{1,0:T(8,128)(2,1)}, u32[]{:S(2)}) copy-start(bf16[4096,256]{1,0:T(8,128)(2,1)} %all-gather.3.cloned.1.call-done) | copy-start | bytes 6291460
Sparse Core Ops, SparseCore 0:
  9.2 39.0 all-gather.4
  50.9 84.9 all-gather.2
  140.0 204.8 reduce-scatter.4
  347.4 70.9 reduce-scatter.2
where the time goes:
time: 428 us; the launch traced here: 427 us
  waiting for transfers between devices  204 us (48%)
  other arithmetic  105 us (25%)
  local copies, waits for them, and re-layouts  56.6 us (13%)
  matrix products  47 us (11%)
  between operations  13.2 us (3%)
    reduce_scatter x1, waiting for transfers between devices, per_device(): lax.psum_scatter(forward, 'col', scatter_dimension=0, tiled=True)  73.6 us
    scatter-add x1, other arithmetic, forward_part(): total = total + jax.ops.segment_sum(far_out, far_local, num_segments=groups)  72.1 us
    reduce_scatter x1, waiting for transfers between devices, per_device(): lax.psum_scatter(backward, 'row', scatter_dimension=0, tiled=True)  51.1 us
    all_gather x1, waiting for transfers between devices, per_device(): col_slab = lax.all_gather(panel_values, 'row', axis=0, tiled=True)  39.2 us
    all_gather x1, waiting for transfers between devices, per_device(): row_slab = lax.all_gather(panel_values, 'col', axis=0, tiled=True)  38.9 us
    reshape x1, local copies, waits for them, and re-layouts, forward_part(): far_out = far_out.reshape(count * LPC, TILE, NRHS)  33.5 us
    scatter-add x1, other arithmetic, forward_part(): total = jax.ops.segment_sum(near_out, near_local, num_segments=groups)  18.2 us
    dot_general x1, matrix products, back_part(): jnp.einsum('skt,skn->stn', far_right, coef, preferred_element_type=jnp.fl...  16.6 us
  transfers between devices with their start and end apart: 4, of which 4 were waited for; matrix products, arithmetic and copies ran while one was open for 49% of the time, Pallas kernels for 0%

commit v1 on v0

--- a/solution.py
+++ b/solution.py
@@ -52,7 +52,10 @@
     rowx = row_slab.reshape(groups, TILE, NRHS)
     near_input = jnp.take(rowx, near_local, axis=0)
     far_input = jnp.take(rowx, far_local, axis=0)
-    col_slab = lax.all_gather(panel_values, "row", axis=0, tiled=True)
+    devices = lax.axis_size("row")
+    blocks = jnp.stack([panel_values for _ in range(devices)])
+    blocks = lax.all_to_all(blocks, "row", split_axis=0, concat_axis=0)
+    col_slab = jnp.concatenate(blocks, axis=0)
     colx = col_slab.reshape(colcount, TILE, NRHS)
     forward = forward_part(
         near_tiles, far_left, far_right, near_local, far_local, colx, colcount, groups

time: 428 us -> 411 us (0.960)
  waiting for transfers between devices: 204 us -> 108 us
  blocking collectives: 0 us -> 75.1 us
    all_to_all x0 -> x1, blocking collectives: none -> 75.1 us  [per_device(): blocks = lax.all_to_all(blocks, 'row', split_axis=0, concat_axis=0)]
    reduce_scatter x1, waiting for transfers between devices: 51.1 us -> 0.02 us  [per_device(): lax.psum_scatter(backward, 'row', scatter_dimension=0, tiled=True)]
    all_gather x1 -> x0, waiting for transfers between devices: 39.2 us -> none  [per_device(): col_slab = lax.all_gather(panel_values, 'row', axis=0, tiled=True)]
    reduce_scatter x1, waiting for transfers between devices: 73.6 us -> 67.5 us  [per_device(): lax.psum_scatter(forward, 'col', scatter_dimension=0, tiled=True)]
  transfers between devices with their start and end apart: 4 -> 3, of which waited for: 4 -> 2; matrix products, arithmetic and copies ran while one was open for 49% -> 40% of each run, Pallas kernels for 0% -> 0%
where the time goes in v1:
time: 411 us; the launch traced here: 410 us
  waiting for transfers between devices  108 us (26%)
  other arithmetic  105 us (26%)
  blocking collectives  75.1 us (18%)
  local copies, waits for them, and re-layouts  57.5 us (14%)
  matrix products  50.9 us (12%)
  between operations  13.1 us (3%)
    all_to_all x1, blocking collectives, per_device(): blocks = lax.all_to_all(blocks, 'row', split_axis=0, concat_axis=0)  75.1 us
    scatter-add x1, other arithmetic, forward_part(): total = total + jax.ops.segment_sum(far_out, far_local, num_segments=groups)  71.8 us
    reduce_scatter x1, waiting for transfers between devices, per_device(): lax.psum_scatter(forward, 'col', scatter_dimension=0, tiled=True)  67.5 us
    all_gather x1, waiting for transfers between devices, per_device(): row_slab = lax.all_gather(panel_values, 'col', axis=0, tiled=True)  39.6 us
    reshape x1, local copies, waits for them, and re-layouts, forward_part(): far_out = far_out.reshape(count * LPC, TILE, NRHS)  33.5 us
    dot_general x1, matrix products, forward_part(): jnp.einsum('cdkt,cdkn->cdtn', left, coef, preferred_element_type=jnp.floa...  20.4 us
    scatter-add x1, other arithmetic, forward_part(): total = jax.ops.segment_sum(near_out, near_local, num_segments=groups)  18.3 us
    dot_general x1, matrix products, back_part(): jnp.einsum('skt,skn->stn', far_right, coef, preferred_element_type=jnp.fl...  16.5 us
  transfers between devices with their start and end apart: 3, of which 2 were waited for; matrix products, arithmetic and copies ran while one was open for 40% of the time, Pallas kernels for 0%

profile of v1, /device:TPU:32, one launch (start us, length us, event | category | flops | bytes accessed | tf_op | source)
XLA Modules:
  0.0 409.8 jit_solution(4730845123740757307)
XLA Ops:
  6.5 0.0 all-gather.2.cloned.1.call-start
  6.5 0.7 all-gather.2.cloned.1.call-update
  7.3 0.0 reduce-scatter.5.cloned.1.call-start
  7.3 0.7 compare_and_fusion
  8.0 0.7 compare_and_fusion.1
  8.7 39.6 %all-gather.2.cloned.1.call-done = bf16[4096,256]{1,0:T(8,128)(2,1)} async-done(((bf16[256,256]{1,0:T(8,128)(2,1)}), bf16[4096,256]{1,0:T(8,128)(2,1)}) %all-gather.2.cloned.1.call-update) | async-done | bytes 2097168 | tf_op jit(solution)/shard_map/all_gather | solution.py:51
  48.3 0.0 copy-start
  48.3 10.0 %gather_fusion.1 = bf16[128,256,256]{2,1,0:T(8,128)(2,1)} fusion(bf16[16,256,256]{2,1,0:T(8,128)(2,1)} %bitcast.33, s32[1024]{0:T(1024)S(1)} %pad_clamp_fusion), kind=kCustom, calls=%fused_computation.1 | custom fusion | bytes 33554944 | tf_op jit(solution)/shard_map/jit(_take)/gather | solution.py:54
  58.3 0.0 copy-done
  58.3 2.8 gather_fusion
  61.1 7.3 %bitcast_reduce_fusion.1 = f32[16,256,256]{1,2,0:T(8,128)} fusion(bf16[32,256,256]{2,1,0:T(8,128)(2,1)} %param.7, bf16[32,256,256]{2,1,0:T(8,128)(2,1)} %gather_fusion, pred[32]{0:T(512)(128)(4,1)S(1)} %get-tuple-element.7), kind=kOutput, calls=%fused_computation.8 | convolution fusion | flops 1076887552 | bytes 12582944 | tf_op jit(solution)/shard_map/sij,sin->sjn/dot_general | solution.py:14
  68.4 16.5 %bitcast_reduce_fusion = f32[16,256,256]{1,2,0:T(8,128)} fusion(bf16[128,64,256]{2,1,0:T(8,128)(2,1)} %param.9, bf16[128,64,256]{2,1,0:T(8,128)(2,1)} %param.8, bf16[128,256,256]{2,1,0:T(8,128)(2,1)} %gather_fusion.1, pred[128]{0:T(512)(128)(4,1)S(1)} %get-tuple-element.5), kind=kOutput, calls=%fused_computation.4 | convolution fusion | flops 2165309440 | bytes 29360256 | tf_op jit(solution)/shard_map/skt,skn->stn/dot_general | solution.py:21
  84.9 6.0 %add.42 = f32[16,256,256]{1,2,0:T(8,128)} add(f32[16,256,256]{1,2,0:T(8,128)} %bitcast_reduce_fusion.1, f32[16,256,256]{1,2,0:T(8,128)} %bitcast_reduce_fusion) | non-fusion elementwise | flops 1048576 | bytes 12582912 | tf_op jit(solution)/shard_map/add | solution.py:23
  90.9 5.3 %copy.13 = f32[16,256,256]{2,1,0:T(8,128)} copy(f32[16,256,256]{1,2,0:T(8,128)} %add.42) | data formatting | bytes 8388608 | tf_op jit(solution)/shard_map/add | solution.py:23
  96.2 0.0 copy-start.1
  96.2 0.0 reduce-scatter.5.cloned.1.call-update
  96.3 0.0 reduce-scatter.3.cloned.1.call-start
  96.3 0.8 copy-done.1
  97.2 0.2 stack.2
  97.4 75.1 %all_to_all.5 = bf16[16,256,256]{2,1,0:T(8,128)(2,1)S(1)} all-to-all(bf16[16,256,256]{2,1,0:T(8,128)(2,1)S(1)} %stack.2), channel_id=1, replica_groups=mesh['row'=16,'col'=16] {'row'}, dimensions={0} | all-to-all | bytes 4194304 | tf_op jit(solution)/shard_map/all_to_all | solution.py:57
  172.4 20.4 %fusion.16 = f32[16,8,256,256]{3,2,1,0:T(8,128)} fusion(bf16[16,8,64,256]{3,2,1,0:T(8,128)(2,1)} %bitcast.40, bf16[16,8,64,256]{3,2,1,0:T(8,128)(2,1)} %bitcast.39, bf16[16,256,256]{2,1,0:T(8,128)(2,1)S(1)} %all_to_all.5), kind=kOutput, calls=%fused_computation.14 | convolution fusion | flops 2149580800 | bytes 44040192 | tf_op jit(solution)/shard_map/cdkt,cdkn->cdtn/dot_general | solution.py:35
  192.8 33.5 %copy.11 = f32[128,256,256]{2,1,0:T(8,128)} copy(f32[128,256,256]{1,2,0:T(8,128)} %bitcast.32) | data formatting | bytes 67108864 | tf_op jit(solution)/shard_map/reshape | solution.py:36
  226.3 2.5 broadcast.11.clone.1
  228.8 71.8 %scatter_fusion.1 = f32[16,256,256]{2,1,0:T(8,128)} fusion(f32[16,256,256]{2,1,0:T(8,128)} %broadcast.11.clone.1, s32[128]{0:T(128)S(1)} %get-tuple-element.6, f32[128,256,256]{2,1,0:T(8,128)} %copy.11), kind=kCustom, calls=%fused_computation.3 | custom fusion | flops 8388608 | bytes 100663808 | tf_op jit(solution)/shard_map/scatter-add | solution.py:38
  300.6 6.7 %fusion.23 = f32[16,2,256,256]{3,2,1,0:T(8,128)} fusion(bf16[16,2,256,256]{3,2,1,0:T(8,128)(2,1)} %bitcast.38, bf16[16,256,256]{2,1,0:T(8,128)(2,1)S(1)} %all_to_all.5), kind=kOutput, calls=%fused_computation.19 | convolution fusion | flops 1073741824 | bytes 14680064 | tf_op jit(solution)/shard_map/cdij,cjn->cdin/dot_general | solution.py:28
  307.3 2.4 broadcast.11.clone
  309.7 18.3 %scatter_fusion = f32[16,256,256]{2,1,0:T(8,128)} fusion(f32[16,256,256]{2,1,0:T(8,128)} %broadcast.11.clone, s32[32]{0:T(128)S(1)} %get-tuple-element.8, f32[32,256,256]{2,1,0:T(8,128)} %bitcast.35), kind=kCustom, calls=%fused_computation.2 | custom fusion | flops 2097152 | bytes 25165952 | tf_op jit(solution)/shard_map/scatter-add | solution.py:37
  328.0 6.0 %add.37 = f32[16,256,256]{2,1,0:T(8,128)} add(f32[16,256,256]{2,1,0:T(8,128)} %scatter_fusion, f32[16,256,256]{2,1,0:T(8,128)} %scatter_fusion.1) | non-fusion elementwise | flops 1048576 | bytes 12582912 | tf_op jit(solution)/shard_map/add | solution.py:38
  334.0 0.0 reduce-scatter.3.cloned.1.call-update
  334.1 0.0 reduce-scatter.5.cloned.1.call-done
  334.1 67.5 %reduce-scatter.3.cloned.1.call-done = f32[256,256]{1,0:T(8,128)} async-done(((f32[4096,256]{1,0:T(8,128)}), f32[256,256]{1,0:T(8,128)}) %reduce-scatter.3.cloned.1.call-update) | async-done | bytes 262160 | tf_op jit(solution)/shard_map/reduce_scatter | solution.py:65
  401.5 1.7 add_convert_fusion
  (4 shorter events, 0.0 us)
Async XLA Ops:
  6.5 41.8 %all-gather.2.cloned.1.call-start = ((), (), s32[]{:S(2)}) async-start(), calls=%async_computation.4 | async-start | bytes 2228224 | tf_op jit(solution)/shard_map/all_gather | solution.py:51
  7.3 326.8 %reduce-scatter.5.cloned.1.call-start = ((), (), s32[]{:S(2)}) async-start(), calls=%async_computation.5 | async-start | bytes 4456448 | tf_op jit(solution)/shard_map/reduce_scatter | solution.py:64
  48.3 10.0 %copy-start = (bf16[4096,256]{1,0:T(8,128)(2,1)S(1)}, bf16[4096,256]{1,0:T(8,128)(2,1)}, u32[]{:S(2)}) copy-start(bf16[4096,256]{1,0:T(8,128)(2,1)} %all-gather.2.cloned.1.call-done) | copy-start | bytes 6291460
  96.2 0.9 copy-start.1
  96.3 305.3 %reduce-scatter.3.cloned.1.call-start = ((), (), s32[]{:S(2)}) async-start(), calls=%async_computation.3 | async-start | bytes 4456448 | tf_op jit(solution)/shard_map/reduce_scatter | solution.py:65
Sparse Core Ops, SparseCore 0:
  9.2 39.0 all-gather.1
  96.4 228.4 reduce-scatter.4
  334.2 67.3 reduce-scatter.2
